TPU v7x, 32 devices: a whole 2x2x4 slice. The times are simulated.
32 devices in a mesh: groups: 2 (over x), dp: 16 (over z, y, core).
Axes of the slice: x: 2, y: 2, z: 4, core: 2. Of those that a mesh axis runs over, the one named last changes fastest.
Arguments:
- inputs: bfloat16 [64, 128, 4096], P(('groups', 'dp')), parts along dimension 0, may hold values from -6 to 6
- outputs: bfloat16 [64, 128, 4096], P(('groups', 'dp')), parts along dimension 0, may hold values from -6 to 6
- lengths: int32 [64], P(('groups', 'dp')), parts along dimension 0, may hold values from 64 to 128
- labels: int32 [64], P(('groups', 'dp')), parts along dimension 0, may hold values from 0 to 13
- norm_gain: float32 [4096], replicated, may hold values from 0.1 to 1.9
- classifier: bfloat16 [4096, 14], replicated, may hold values from -0.09375 to 0.09375
- proj_in: bfloat16 [4096, 64], replicated, may hold values from -0.09375 to 0.09375
- proj_out: bfloat16 [4096, 128], replicated, may hold values from -0.09375 to 0.09375
- query_index: int32 [256], P('groups'), parts along dimension 0, may hold values from 0 to 31, as said below
- prior_fisher: float32 [16384, 8192], P('groups', 'dp'), parts along dimension 0, may hold values from -4 to 18, as said below
Outputs:
- influence: float32 [8192, 256], P('dp', 'groups'), parts along dimension 1
- scores: float32 [64, 128], P(('groups', 'dp')), parts along dimension 0
There are 2 independent parts, one for each index of `groups`. A program takes and returns all parts, laid end to end along the dimension named above; an argument that names none is the same for every part. Nothing has to cross between parts.
Inputs may be any that keep to these rules, and one draw needn't show every extreme that they name: `query_index`: indices may repeat. `prior_fisher`: symmetric and positive definite.
All inputs are finite; a program needn't handle non-finite values.
Results may differ from a plain program's by a relative error of at most 0.0044.
Values may be sent and summed in bfloat16 or wider, within the bound.
A program may use at most 128 MiB of HBM per device.

v0:
```python
import jax
import jax.numpy as jnp
from jax import lax
from jax.sharding import PartitionSpec as P

D = 4096
CLASSES = 14
ITERS = 4
norm_eps = 1e-05
damp_share = 0.5
highest = lax.Precision.HIGHEST


def project_rows(inputs, outputs, lengths, labels, norm_gain, classifier, proj_in, proj_out):
    ex_count = inputs.shape[0]
    tok_count = inputs.shape[1]
    hidden = outputs.astype(jnp.float32)
    root_mean = jnp.sqrt(jnp.mean(hidden * hidden, axis=-1, keepdims=True) + norm_eps)
    positions = jnp.arange(tok_count, dtype=jnp.int32)
    live_mask = (positions[None, :] < lengths[:, None]).astype(jnp.float32)[:, :, None]
    length_float = lengths.astype(jnp.float32)[:, None, None]
    normed = norm_gain * hidden / root_mean
    pooled = jnp.sum(live_mask * normed, axis=1) / length_float[:, 0]
    class_weight = classifier.astype(jnp.float32)
    logits = jnp.dot(pooled, class_weight, precision=highest)
    exponent = jnp.exp(logits)
    probs = exponent / jnp.sum(exponent, axis=-1, keepdims=True)
    target = (jnp.arange(CLASSES, dtype=jnp.int32)[None, :] == labels[:, None]).astype(jnp.float32)
    pooled_grad = lax.dot_general(
        probs - target, class_weight, (((1,), (1,)), ((), ())), precision=highest
    )
    scaled = norm_gain * (live_mask / length_float) * pooled_grad[:, None, :]
    out_grad = scaled / root_mean - hidden * jnp.sum(hidden * scaled, axis=-1, keepdims=True) / (
        D * root_mean**3
    )
    grad_low = out_grad.astype(jnp.bfloat16)
    input_proj = jnp.dot(
        inputs.reshape(ex_count * tok_count, D).astype(jnp.float32),
        proj_in.astype(jnp.float32),
        precision=highest,
    )
    grad_proj = jnp.dot(
        grad_low.reshape(ex_count * tok_count, D).astype(jnp.float32),
        proj_out.astype(jnp.float32),
        precision=highest,
    )
    input_proj = input_proj.reshape(ex_count, tok_count, -1)
    grad_proj = grad_proj.reshape(ex_count, tok_count, -1)
    outer = jnp.einsum("eta,etb->eab", input_proj, grad_proj, precision=highest)
    return outer.reshape(ex_count, -1).astype(jnp.bfloat16)


def conjugate(queries, apply_fisher, reduce_inner):
    solved = jnp.zeros_like(queries)
    residual = queries
    direction = queries
    norm_now = reduce_inner(residual, residual)
    for step_index in range(ITERS):
        image = apply_fisher(direction)
        alpha = norm_now / reduce_inner(direction, image)
        solved = solved + alpha * direction
        residual = residual - alpha * image
        norm_next = reduce_inner(residual, residual)
        direction = residual + norm_next / norm_now * direction
        norm_now = norm_next
    return solved


def pieces_inner(first_vec, second_vec):
    return lax.psum(jnp.sum(first_vec * second_vec, axis=0), "dp")


def contract_rows(left_rows, right_rows):
    return jnp.dot(
        left_rows.astype(jnp.float32).T, right_rows.astype(jnp.float32), precision=highest
    )


def body(
    inputs,
    outputs,
    lengths,
    labels,
    norm_gain,
    classifier,
    proj_in,
    proj_out,
    query_index,
    prior_fisher,
):
    own_rows = project_rows(
        inputs, outputs, lengths, labels, norm_gain, classifier, proj_in, proj_out
    )
    devices = lax.axis_size("dp")
    device_index = lax.axis_index("dp")
    own_count = own_rows.shape[0]
    total_rows = own_count * devices
    width = own_rows.shape[1]
    piece = width // devices
    own_float = own_rows.astype(jnp.float32)
    square_sum = lax.psum(jnp.sum(own_float * own_float), "dp")
    damping = damp_share * square_sum / (total_rows * total_rows)
    every = lax.all_gather(own_rows, "dp", axis=0, tiled=True)
    mine = lax.dynamic_slice_in_dim(every, device_index * piece, piece, 1)
    strip = contract_rows(every, mine) / total_rows + damping * prior_fisher

    def apply_piece(vectors):
        return lax.psum_scatter(
            jnp.dot(strip, vectors, precision=highest), "dp", scatter_dimension=0, tiled=True
        )

    queries = jnp.take(mine, query_index, axis=0).astype(jnp.float32).T
    solved = conjugate(queries, apply_piece, pieces_inner)
    block = mine.astype(jnp.float32)
    scores = lax.psum_scatter(
        jnp.dot(block, solved, precision=highest) / total_rows,
        "dp",
        scatter_dimension=0,
        tiled=True,
    )
    return (solved, scores)


def solution(mesh):
    return jax.shard_map(
        body,
        mesh=mesh,
        in_specs=(
            P(("groups", "dp"), None, None),
            P(("groups", "dp"), None, None),
            P(("groups", "dp")),
            P(("groups", "dp")),
            P(),
            P(),
            P(),
            P(),
            P("groups"),
            P("groups", "dp"),
        ),
        out_specs=(P("dp", "groups"), P(("groups", "dp"), None)),
        check_vma=False,
    )
```

profile of v0, /device:TPU:0, one launch (start us, length us, event | category | flops | bytes accessed | tf_op | source)
XLA Modules:
  0.0 715.0 jit_solution(6194514816210829395)
XLA Ops:
  7.2 0.0 copy-start
  7.2 0.0 copy-start.7
  7.2 0.0 reduce-scatter.5.cloned.1.call-start
  7.3 0.0 copy-start.3
  7.3 0.8 convert_element_type.49
  8.1 0.8 compare_convert_fusion.1
  8.9 0.7 compare_select_fusion
  9.6 0.7 compare_and_fusion
  10.2 2.1 fusion.6
  12.3 0.7 add_sqrt_fusion
  13.1 2.5 fusion.8
  15.6 0.4 fusion.33
  16.0 0.3 fusion.25
  16.3 0.0 copy-start.4
  16.3 0.0 copy-start.6
  16.3 2.1 fusion.3
  18.4 0.7 fusion.12
  19.2 0.8 fusion.14
  19.9 0.8 multiply_reduce_fusion.6
  20.8 24.6 %all-gather = bf16[16,2,8192]{2,1,0:T(2,128)(2,1)S(1)} all-gather(bf16[1,2,8192]{2,1,0:T(2,128)(2,1)S(1)} %reshape.115), channel_id=1, replica_groups=mesh['groups'=2,'dp'=16] {'dp'}, dimensions={0}, use_global_device_ids=true | all-gather | bytes 557056 | tf_op jit(solution)/shard_map/all_gather | solution.py:103
  45.4 0.2 reshape.116
  45.6 30.5 %psum.64 = f32[]{:T(128)} all-reduce(f32[]{:T(128)} %get-tuple-element.12), channel_id=1, replica_groups=mesh['groups'=2,'dp'=16] {'dp'}, use_global_device_ids=true, to_apply=%region_7.8 | all-reduce | flops 1 | bytes 8 | tf_op jit(solution)/shard_map/psum | solution.py:101
  76.1 0.8 gather_fusion
  76.9 0.1 copy.13
  77.7 8.1 %multiply_add_fusion = f32[8192,512]{1,0:T(8,128)S(1)} fusion(f32[8192,512]{1,0:T(8,128)} %param.19, bf16[32,8192]{1,0:T(8,128)(2,1)S(1)} %reshape.116, bf16[32,512]{1,0:T(8,128)(2,1)S(1)} %constant_dynamic-slice_fusion.1, f32[]{:T(128)S(6)} %div.104), kind=kOutput, calls=%fused_computation.2 | convolution fusion | flops 281018368 | bytes 34111492 | tf_op jit(solution)/shard_map/dot_general | solution.py:74
  85.9 5.7 copy-done.1
  91.6 9.1 %fusion.22 = f32[8192,128]{1,0:T(8,128)} fusion(f32[8192,512]{1,0:T(8,128)S(1)} %multiply_add_fusion, bf16[128,512]{0,1:T(8,128)(2,1)S(1)} %copy.13, pred[128]{0:T(512)(128)(4,1)S(1)} %compare_and_fusion), kind=kOutput, calls=%fused_computation.49 | convolution fusion | flops 6442516480 | bytes 21102720 | tf_op jit(solution)/shard_map/dot_general | solution.py:109
  100.7 0.0 reduce-scatter.5.cloned.1.call-update
  100.7 0.0 reduce-scatter.7.cloned.1.call-start
  100.7 69.7 %reduce-scatter.5.cloned.1.call-done = f32[512,128]{1,0:T(8,128)} async-done(((f32[8192,128]{1,0:T(8,128)}), f32[512,128]{1,0:T(8,128)}) %reduce-scatter.5.cloned.1.call-update) | async-done | bytes 262160 | tf_op jit(solution)/shard_map/reduce_scatter | solution.py:108
  170.5 1.0 fusion.17
  171.5 30.4 %all-reduce.1 = (f32[128]{0:T(128)S(1)}, f32[128]{0:T(128)S(1)}) all-reduce(f32[128]{0:T(128)S(1)} %get-tuple-element.3, f32[128]{0:T(128)S(1)} %get-tuple-element.2), channel_id=1, replica_groups=mesh['groups'=2,'dp'=16] {'dp'}, use_global_device_ids=true, to_apply=%region_5.0 | all-reduce | flops 256 | bytes 2048 | tf_op jit(solution)/shard_map/psum | solution.py:70
  201.9 1.0 multiply_reduce_fusion.5
  202.9 29.5 %psum.66 = f32[128]{0:T(128)S(1)} all-reduce(f32[128]{0:T(128)S(1)} %multiply_reduce_fusion.5), channel_id=1, replica_groups=mesh['groups'=2,'dp'=16] {'dp'}, use_global_device_ids=true, to_apply=%region_12.13 | all-reduce | flops 128 | bytes 1024 | tf_op jit(solution)/shard_map/psum | solution.py:70
  232.4 17.4 %fusion.31 = f32[8192,128]{1,0:T(8,128)} fusion(f32[8192,512]{1,0:T(8,128)} %copy-done.1, f32[512,128]{1,0:T(8,128)} %reduce-scatter.5.cloned.1.call-done, f32[128]{0:T(128)S(1)} %div.106, f32[128]{0:T(128)S(1)} %div.105, bf16[128,512]{0,1:T(8,128)(2,1)S(1)} %copy.13, pred[128]{0:T(512)(128)(4,1)S(1)} %compare_and_fusion), kind=kOutput, calls=%fused_computation.69 | convolution fusion | flops 6442844160 | bytes 21365888 | tf_op jit(solution)/shard_map/dot_general | solution.py:109
  249.8 0.0 reduce-scatter.7.cloned.1.call-update
  249.8 0.0 reduce-scatter.9.cloned.1.call-start
  249.9 69.6 %reduce-scatter.7.cloned.1.call-done = f32[512,128]{1,0:T(8,128)} async-done(((f32[8192,128]{1,0:T(8,128)}), f32[512,128]{1,0:T(8,128)}) %reduce-scatter.7.cloned.1.call-update) | async-done | bytes 262160 | tf_op jit(solution)/shard_map/reduce_scatter | solution.py:108
  319.5 1.0 multiply_reduce_fusion.4
  320.6 30.1 %psum.67 = f32[128]{0:T(128)S(1)} all-reduce(f32[128]{0:T(128)S(1)} %multiply_reduce_fusion.4), channel_id=1, replica_groups=mesh['groups'=2,'dp'=16] {'dp'}, use_global_device_ids=true, to_apply=%region_15.16 | all-reduce | flops 128 | bytes 1024 | tf_op jit(solution)/shard_map/psum | solution.py:70
  350.7 1.0 multiply_reduce_fusion.3
  351.8 29.5 %psum.68 = f32[128]{0:T(128)S(1)} all-reduce(f32[128]{0:T(128)S(1)} %get-tuple-element.6), channel_id=1, replica_groups=mesh['groups'=2,'dp'=16] {'dp'}, use_global_device_ids=true, to_apply=%region_17.18 | all-reduce | flops 128 | bytes 1024 | tf_op jit(solution)/shard_map/psum | solution.py:70
  381.3 0.1 multiply_add_fusion.2
  381.4 17.4 %fusion.34 = f32[8192,128]{1,0:T(8,128)} fusion(f32[8192,512]{1,0:T(8,128)} %copy-done.1, f32[512,128]{1,0:T(8,128)S(1)} %multiply_add_fusion.2), kind=kOutput, calls=%fused_computation.71 | convolution fusion | flops 6442450944 | bytes 21233664 | tf_op jit(solution)/shard_map/dot_general | solution.py:109
  398.8 0.0 reduce-scatter.9.cloned.1.call-update
  398.8 0.0 reduce-scatter.11.cloned.1.call-start
  398.8 69.7 %reduce-scatter.9.cloned.1.call-done = f32[512,128]{1,0:T(8,128)} async-done(((f32[8192,128]{1,0:T(8,128)}), f32[512,128]{1,0:T(8,128)}) %reduce-scatter.9.cloned.1.call-update) | async-done | bytes 262160 | tf_op jit(solution)/shard_map/reduce_scatter | solution.py:108
  468.6 1.0 multiply_reduce_fusion.2
  469.6 30.1 %psum.69 = f32[128]{0:T(128)S(1)} all-reduce(f32[128]{0:T(128)S(1)} %multiply_reduce_fusion.2), channel_id=1, replica_groups=mesh['groups'=2,'dp'=16] {'dp'}, use_global_device_ids=true, to_apply=%region_20.21 | all-reduce | flops 128 | bytes 1024 | tf_op jit(solution)/shard_map/psum | solution.py:70
  499.7 1.0 multiply_reduce_fusion.1
  500.8 29.7 %psum.70 = f32[128]{0:T(128)S(1)} all-reduce(f32[128]{0:T(128)S(1)} %multiply_reduce_fusion.1), channel_id=1, replica_groups=mesh['groups'=2,'dp'=16] {'dp'}, use_global_device_ids=true, to_apply=%region_22.23 | all-reduce | flops 128 | bytes 1024 | tf_op jit(solution)/shard_map/psum | solution.py:70
  530.5 1.0 multiply_add_fusion.1
  531.5 17.4 %fusion.35 = f32[8192,128]{1,0:T(8,128)} fusion(f32[8192,512]{1,0:T(8,128)} %copy-done.1, f32[512,128]{1,0:T(8,128)S(1)} %multiply_add_fusion.1), kind=kOutput, calls=%fused_computation.72 | convolution fusion | flops 6442450944 | bytes 21233664 | tf_op jit(solution)/shard_map/dot_general | solution.py:109
  548.9 0.0 reduce-scatter.11.cloned.1.call-update
  548.9 0.6 copy-done.10
  549.6 0.6 dynamic-slice
  550.8 68.0 %reduce-scatter.11.cloned.1.call-done = f32[512,128]{1,0:T(8,128)} async-done(((f32[8192,128]{1,0:T(8,128)}), f32[512,128]{1,0:T(8,128)}) %reduce-scatter.11.cloned.1.call-update) | async-done | bytes 262160 | tf_op jit(solution)/shard_map/reduce_scatter | solution.py:108
  618.8 1.0 multiply_reduce_fusion
  619.9 30.1 %psum.71 = f32[128]{0:T(128)S(1)} all-reduce(f32[128]{0:T(128)S(1)} %multiply_reduce_fusion), channel_id=1, replica_groups=mesh['groups'=2,'dp'=16] {'dp'}, use_global_device_ids=true, to_apply=%region_25.26 | all-reduce | flops 128 | bytes 1024 | tf_op jit(solution)/shard_map/psum | solution.py:70
  649.9 0.1 fusion.20
  650.0 0.0 copy-start.5
  650.1 0.2 convolution_multiply_fusion
  650.3 57.6 %all-reduce = f32[32,128]{1,0:T(8,128)S(1)} all-reduce(f32[32,128]{1,0:T(8,128)S(1)} %convolution_multiply_fusion), channel_id=6, replica_groups=mesh['groups'=2,'dp'=16] {'dp'}, use_global_device_ids=true, to_apply=%region_26.27.clone | all-reduce | flops 4096 | bytes 32768
  707.9 0.6 constant_dynamic-slice_fusion
  (24 shorter events, 0.1 us)
Async XLA Ops:
  7.2 12.0 %copy-start = (bf16[2,128,4096]{2,1,0:T(8,128)(2,1)S(1)}, bf16[2,128,4096]{2,1,0:T(8,128)(2,1)}, u32[]{:S(2)}) copy-start(bf16[2,128,4096]{2,1,0:T(8,128)(2,1)} %param.10) | copy-start | bytes 6291460
  7.2 9.1 %copy-start.7 = (f32[4096]{0:T(1024)S(1)}, f32[4096]{0:T(1024)}, u32[]{:S(2)}) copy-start(f32[4096]{0:T(1024)} %param.14) | copy-start | bytes 49156
  7.2 8.4 %copy-start.8 = (bf16[4096,14]{0,1:T(8,128)(2,1)S(1)}, bf16[4096,14]{0,1:T(8,128)(2,1)}, u32[]{:S(2)}) copy-start(bf16[4096,14]{0,1:T(8,128)(2,1)} %param.15) | copy-start | bytes 344068
  7.2 8.8 %copy-start.9 = (s32[2]{0:T(128)S(1)}, s32[2]{0:T(128)}, u32[]{:S(2)}) copy-start(s32[2]{0:T(128)} %param.13) | copy-start | bytes 28
  7.2 163.2 %reduce-scatter.5.cloned.1.call-start = ((), (), s32[]{:S(2)}) async-start(), calls=%async_computation.4 | async-start | bytes 4456448 | tf_op jit(solution)/shard_map/reduce_scatter | solution.py:108
  7.3 9.1 %copy-start.3 = (bf16[2,128,4096]{2,1,0:T(8,128)(2,1)S(1)}, bf16[2,128,4096]{2,1,0:T(8,128)(2,1)}, u32[]{:S(2)}) copy-start(bf16[2,128,4096]{2,1,0:T(8,128)(2,1)} %param.11) | copy-start | bytes 6291460
  16.3 2.1 copy-start.4
  16.3 2.8 copy-start.6
  85.8 5.7 copy-start.1
  100.7 218.9 %reduce-scatter.7.cloned.1.call-start = ((), (), s32[]{:S(2)}) async-start(), calls=%async_computation.5 | async-start | bytes 4456448 | tf_op jit(solution)/shard_map/reduce_scatter | solution.py:108
  249.8 69.7 %copy-start.2 = (f32[512,128]{1,0:T(8,128)S(1)}, f32[512,128]{1,0:T(8,128)}, u32[]{:S(2)}) copy-start(f32[512,128]{1,0:T(8,128)} %reduce-scatter.5.cloned.1.call-done) | copy-start | bytes 786436
  249.8 218.7 %reduce-scatter.9.cloned.1.call-start = ((), (), s32[]{:S(2)}) async-start(), calls=%async_computation.6 | async-start | bytes 4456448 | tf_op jit(solution)/shard_map/reduce_scatter | solution.py:108
  398.8 220.0 %reduce-scatter.11.cloned.1.call-start = ((), (), s32[]{:S(2)}) async-start(), calls=%async_computation.7 | async-start | bytes 4456448 | tf_op jit(solution)/shard_map/reduce_scatter | solution.py:108
  548.9 0.7 copy-start.10
  650.0 58.4 %copy-start.5 = (f32[512,128]{1,0:T(8,128)}, f32[512,128]{1,0:T(8,128)S(1)}, u32[]{:S(2)}) copy-start(f32[512,128]{1,0:T(8,128)S(1)} %fusion.20) | copy-start | bytes 786436
Sparse Core Ops, SparseCore 0:
  100.8 69.6 reduce-scatter.4
  250.0 69.5 reduce-scatter.6
  398.9 69.6 reduce-scatter.8
  549.1 69.7 reduce-scatter.10
where the time goes:
time: 716 us; the launch traced here: 715 us
  blocking collectives  322 us (45%)
  waiting for transfers between devices  277 us (39%)
  matrix products  72.7 us (10%)
  other arithmetic  18.8 us (3%)
  between operations  15.3 us (2%)
  local copies, waits for them, and re-layouts  8.71 us (1%)
    reduce_scatter x4, waiting for transfers between devices, apply_piece(): lax.psum_scatter(jnp.dot(strip, vectors, precision=highest), 'dp', scatte...  277 us
    psum x7, blocking collectives, pieces_inner(): return lax.psum(jnp.sum(first_vec * second_vec, axis=0), 'dp')  209 us
    dot_general x4, matrix products, apply_piece(): jnp.dot(strip, vectors, precision=highest)  61.4 us
    unnamed x1, blocking collectives  57.6 us
    psum x1, blocking collectives, body(): square_sum = lax.psum(jnp.sum(own_float * own_float), 'dp')  30.5 us
    all_gather x1, blocking collectives, body(): every = lax.all_gather(own_rows, 'dp', axis=0, tiled=True)  24.6 us
  transfers between devices with their start and end apart: 4, of which 4 were waited for; matrix products, arithmetic and copies ran while one was open for 0% of the time, Pallas kernels for 0%

commit v1 on v0

--- a/solution.py
+++ b/solution.py
@@ -9,6 +9,19 @@
 norm_eps = 1e-05
 damp_share = 0.5
 highest = lax.Precision.HIGHEST
+
+
+def gather_around(value, axis, dim):
+    ways = lax.axis_size(axis)
+    up = [(d, (d + 1) % ways) for d in range(ways)]
+    down = [(d, (d - 1) % ways) for d in range(ways)]
+    earlier, later = ([value], [value])
+    for _ in range(ways // 2):
+        earlier.append(lax.ppermute(earlier[-1], axis, up))
+    for _ in range((ways - 1) // 2):
+        later.append(lax.ppermute(later[-1], axis, down))
+    line = jnp.concatenate([*earlier[::-1], *later[1:]], axis=dim)
+    return jnp.roll(line, (lax.axis_index(axis) - ways // 2) * value.shape[dim], axis=dim)
 
 
 def project_rows(inputs, outputs, lengths, labels, norm_gain, classifier, proj_in, proj_out):
@@ -100,7 +113,7 @@
     own_float = own_rows.astype(jnp.float32)
     square_sum = lax.psum(jnp.sum(own_float * own_float), "dp")
     damping = damp_share * square_sum / (total_rows * total_rows)
-    every = lax.all_gather(own_rows, "dp", axis=0, tiled=True)
+    every = gather_around(own_rows, "dp", 0)
     mine = lax.dynamic_slice_in_dim(every, device_index * piece, piece, 1)
     strip = contract_rows(every, mine) / total_rows + damping * prior_fisher
 

time: 716 us -> 744 us (1.039)
  starting transfers between devices: 0.16 us -> 32.4 us
  blocking collectives: 322 us -> 302 us
  waiting for transfers between devices: 277 us -> 289 us
    ppermute x0 -> x15, starting transfers between devices: none -> 32.2 us  [the longest x7 31.7 us: gather_around(): later.append(lax.ppermute(later[-1], axis, down))]
    all_gather x1 -> x0, blocking collectives: 24.6 us -> none  [body(): every = lax.all_gather(own_rows, 'dp', axis=0, tiled=True)]
    ppermute x0 -> x15, waiting for transfers between devices: none -> 11.1 us  [the longest x8 10.7 us: gather_around(): earlier.append(lax.ppermute(earlier[-1], axis, up))]
  transfers between devices with their start and end apart: 4 -> 19, of which waited for: 4 -> 17; matrix products, arithmetic and copies ran while one was open for 0% -> 0% of each run, Pallas kernels for 0% -> 0%
where the time goes in v1:
time: 744 us; the launch traced here: 743 us
  blocking collectives  302 us (41%)
  waiting for transfers between devices  289 us (39%)
  matrix products  72.8 us (10%)
  starting transfers between devices  32.4 us (4%)
  other arithmetic  17.5 us (2%)
  between operations  15.4 us (2%)
  local copies, waits for them, and re-layouts  13.9 us (2%)
    reduce_scatter x4, waiting for transfers between devices, apply_piece(): lax.psum_scatter(jnp.dot(strip, vectors, precision=highest), 'dp', scatte...  278 us
    psum x7, blocking collectives, pieces_inner(): return lax.psum(jnp.sum(first_vec * second_vec, axis=0), 'dp')  209 us
    dot_general x4, matrix products, apply_piece(): jnp.dot(strip, vectors, precision=highest)  61.4 us
    unnamed x1, blocking collectives  57.6 us
    psum x1, blocking collectives, body(): square_sum = lax.psum(jnp.sum(own_float * own_float), 'dp')  34.7 us
    ppermute x7, starting transfers between devices, gather_around(): later.append(lax.ppermute(later[-1], axis, down))  31.7 us
  transfers between devices with their start and end apart: 19, of which 17 were waited for; matrix products, arithmetic and copies ran while one was open for 0% of the time, Pallas kernels for 0%

profile of v1, /device:TPU:0, one launch (start us, length us, event | category | flops | bytes accessed | tf_op | source)
XLA Modules:
  0.0 742.7 jit_solution(4502224137481339887)
XLA Ops:
  7.3 0.8 convert_element_type.49
  8.1 0.8 compare_convert_fusion.1
  8.9 2.1 fusion.6
  11.0 0.7 add_sqrt_fusion
  11.7 2.5 fusion.8
  14.3 0.4 fusion.35
  14.7 0.3 fusion.26
  15.0 2.1 fusion.3
  17.1 0.7 fusion.12
  17.9 0.8 fusion.14
  18.6 0.8 multiply_reduce_fusion.6
  19.5 0.5 collective-permute-start
  20.0 5.1 collective-permute-start.8
  25.1 1.5 collective-permute-done
  26.7 4.4 collective-permute-start.9
  31.1 1.5 collective-permute-done.1
  32.7 4.4 collective-permute-start.10
  37.2 1.5 collective-permute-done.2
  38.8 4.4 collective-permute-start.11
  43.2 1.5 collective-permute-done.3
  44.8 4.4 collective-permute-start.12
  49.2 1.5 collective-permute-done.4
  50.8 4.4 collective-permute-start.13
  55.3 1.5 collective-permute-done.5
  56.9 4.4 collective-permute-start.14
  61.3 1.5 collective-permute-done.6
  62.9 34.7 %psum.64 = f32[]{:T(128)} all-reduce(f32[]{:T(128)} %get-tuple-element.12), channel_id=1, replica_groups=mesh['groups'=2,'dp'=16] {'dp'}, use_global_device_ids=true, to_apply=%region_7.8 | all-reduce | flops 1 | bytes 8 | tf_op jit(solution)/shard_map/psum | solution.py:114
  98.3 0.6 copy-done.9
  98.9 4.7 concatenate.6
  103.6 0.1 dynamic_slice.7
  103.7 0.8 gather_fusion
  104.5 0.1 copy.13
  104.6 8.2 %multiply_add_fusion = f32[8192,512]{1,0:T(8,128)S(1)} fusion(f32[8192,512]{1,0:T(8,128)} %param.19, bf16[32,512]{1,0:T(8,128)(2,1)S(1)} %dynamic_slice.7, f32[]{:T(128)S(6)} %div.104, bf16[64,8192]{1,0:T(8,128)(2,1)S(1)} %concatenate.6, s32[]{:T(128)S(6)} %select_n.33), kind=kOutput, calls=%fused_computation.2 | convolution fusion | flops 281018368 | bytes 34111496 | tf_op jit(solution)/shard_map/dot_general | solution.py:87
  112.8 5.7 copy-done.1
  118.5 9.1 %fusion.23 = f32[8192,128]{1,0:T(8,128)} fusion(f32[8192,512]{1,0:T(8,128)S(1)} %multiply_add_fusion, bf16[128,512]{0,1:T(8,128)(2,1)S(1)} %copy.13, pred[128]{0:T(512)(128)(4,1)S(1)} %compare_and_fusion), kind=kOutput, calls=%fused_computation.50 | convolution fusion | flops 6442516480 | bytes 21102720 | tf_op jit(solution)/shard_map/dot_general | solution.py:122
  127.7 70.3 %reduce-scatter.5.cloned.1.call-done = f32[512,128]{1,0:T(8,128)} async-done(((f32[8192,128]{1,0:T(8,128)}), f32[512,128]{1,0:T(8,128)}) %reduce-scatter.5.cloned.1.call-update) | async-done | bytes 262160 | tf_op jit(solution)/shard_map/reduce_scatter | solution.py:121
  197.9 1.0 fusion.18
  199.0 30.1 %all-reduce.1 = (f32[128]{0:T(128)S(1)}, f32[128]{0:T(128)S(1)}) all-reduce(f32[128]{0:T(128)S(1)} %get-tuple-element.3, f32[128]{0:T(128)S(1)} %get-tuple-element.2), channel_id=1, replica_groups=mesh['groups'=2,'dp'=16] {'dp'}, use_global_device_ids=true, to_apply=%region_5.0 | all-reduce | flops 256 | bytes 2048 | tf_op jit(solution)/shard_map/psum | solution.py:83
  229.0 1.0 multiply_reduce_fusion.5
  230.1 29.7 %psum.66 = f32[128]{0:T(128)S(1)} all-reduce(f32[128]{0:T(128)S(1)} %multiply_reduce_fusion.5), channel_id=1, replica_groups=mesh['groups'=2,'dp'=16] {'dp'}, use_global_device_ids=true, to_apply=%region_12.13 | all-reduce | flops 128 | bytes 1024 | tf_op jit(solution)/shard_map/psum | solution.py:83
  259.8 17.4 %fusion.33 = f32[8192,128]{1,0:T(8,128)} fusion(f32[8192,512]{1,0:T(8,128)} %copy-done.1, f32[512,128]{1,0:T(8,128)} %reduce-scatter.5.cloned.1.call-done, f32[128]{0:T(128)S(1)} %div.106, f32[128]{0:T(128)S(1)} %div.105, bf16[128,512]{0,1:T(8,128)(2,1)S(1)} %copy.13, pred[128]{0:T(512)(128)(4,1)S(1)} %compare_and_fusion), kind=kOutput, calls=%fused_computation.71 | convolution fusion | flops 6442844160 | bytes 21365888 | tf_op jit(solution)/shard_map/dot_general | solution.py:122
  277.3 69.7 %reduce-scatter.7.cloned.1.call-done = f32[512,128]{1,0:T(8,128)} async-done(((f32[8192,128]{1,0:T(8,128)}), f32[512,128]{1,0:T(8,128)}) %reduce-scatter.7.cloned.1.call-update) | async-done | bytes 262160 | tf_op jit(solution)/shard_map/reduce_scatter | solution.py:121
  347.0 1.0 multiply_reduce_fusion.4
  348.0 30.2 %psum.67 = f32[128]{0:T(128)S(1)} all-reduce(f32[128]{0:T(128)S(1)} %multiply_reduce_fusion.4), channel_id=1, replica_groups=mesh['groups'=2,'dp'=16] {'dp'}, use_global_device_ids=true, to_apply=%region_15.16 | all-reduce | flops 128 | bytes 1024 | tf_op jit(solution)/shard_map/psum | solution.py:83
  378.2 1.0 multiply_reduce_fusion.3
  379.2 29.5 %psum.68 = f32[128]{0:T(128)S(1)} all-reduce(f32[128]{0:T(128)S(1)} %get-tuple-element.6), channel_id=1, replica_groups=mesh['groups'=2,'dp'=16] {'dp'}, use_global_device_ids=true, to_apply=%region_17.18 | all-reduce | flops 128 | bytes 1024 | tf_op jit(solution)/shard_map/psum | solution.py:83
  408.7 0.1 multiply_add_fusion.2
  408.8 17.4 %fusion.36 = f32[8192,128]{1,0:T(8,128)} fusion(f32[8192,512]{1,0:T(8,128)} %copy-done.1, f32[512,128]{1,0:T(8,128)S(1)} %multiply_add_fusion.2), kind=kOutput, calls=%fused_computation.73 | convolution fusion | flops 6442450944 | bytes 21233664 | tf_op jit(solution)/shard_map/dot_general | solution.py:122
  426.3 70.0 %reduce-scatter.9.cloned.1.call-done = f32[512,128]{1,0:T(8,128)} async-done(((f32[8192,128]{1,0:T(8,128)}), f32[512,128]{1,0:T(8,128)}) %reduce-scatter.9.cloned.1.call-update) | async-done | bytes 262160 | tf_op jit(solution)/shard_map/reduce_scatter | solution.py:121
  496.3 1.0 multiply_reduce_fusion.2
  497.4 30.1 %psum.69 = f32[128]{0:T(128)S(1)} all-reduce(f32[128]{0:T(128)S(1)} %multiply_reduce_fusion.2), channel_id=1, replica_groups=mesh['groups'=2,'dp'=16] {'dp'}, use_global_device_ids=true, to_apply=%region_20.21 | all-reduce | flops 128 | bytes 1024 | tf_op jit(solution)/shard_map/psum | solution.py:83
  527.4 1.0 multiply_reduce_fusion.1
  528.5 29.7 %psum.70 = f32[128]{0:T(128)S(1)} all-reduce(f32[128]{0:T(128)S(1)} %multiply_reduce_fusion.1), channel_id=1, replica_groups=mesh['groups'=2,'dp'=16] {'dp'}, use_global_device_ids=true, to_apply=%region_22.23 | all-reduce | flops 128 | bytes 1024 | tf_op jit(solution)/shard_map/psum | solution.py:83
  558.2 1.0 multiply_add_fusion.1
  559.2 17.4 %fusion.37 = f32[8192,128]{1,0:T(8,128)} fusion(f32[8192,512]{1,0:T(8,128)} %copy-done.1, f32[512,128]{1,0:T(8,128)S(1)} %multiply_add_fusion.1), kind=kOutput, calls=%fused_computation.74 | convolution fusion | flops 6442450944 | bytes 21233664 | tf_op jit(solution)/shard_map/dot_general | solution.py:122
  576.7 0.6 copy-done.14
  577.3 0.6 dynamic-slice
  578.5 67.9 %reduce-scatter.11.cloned.1.call-done = f32[512,128]{1,0:T(8,128)} async-done(((f32[8192,128]{1,0:T(8,128)}), f32[512,128]{1,0:T(8,128)}) %reduce-scatter.11.cloned.1.call-update) | async-done | bytes 262160 | tf_op jit(solution)/shard_map/reduce_scatter | solution.py:121
  646.4 1.0 multiply_reduce_fusion
  647.5 30.2 %psum.71 = f32[128]{0:T(128)S(1)} all-reduce(f32[128]{0:T(128)S(1)} %multiply_reduce_fusion), channel_id=1, replica_groups=mesh['groups'=2,'dp'=16] {'dp'}, use_global_device_ids=true, to_apply=%region_25.26 | all-reduce | flops 128 | bytes 1024 | tf_op jit(solution)/shard_map/psum | solution.py:83
  677.6 0.1 fusion.21
  677.8 0.2 convolution_multiply_fusion
  678.0 57.6 %all-reduce = f32[32,128]{1,0:T(8,128)S(1)} all-reduce(f32[32,128]{1,0:T(8,128)S(1)} %convolution_multiply_fusion), channel_id=6, replica_groups=mesh['groups'=2,'dp'=16] {'dp'}, use_global_device_ids=true, to_apply=%region_26.27.clone | all-reduce | flops 4096 | bytes 32768
  735.6 0.6 constant_dynamic-slice_fusion
  (61 shorter events, 0.8 us)
Async XLA Ops:
  7.2 10.7 %copy-start = (bf16[2,128,4096]{2,1,0:T(8,128)(2,1)S(1)}, bf16[2,128,4096]{2,1,0:T(8,128)(2,1)}, u32[]{:S(2)}) copy-start(bf16[2,128,4096]{2,1,0:T(8,128)(2,1)} %param.10) | copy-start | bytes 6291460
  7.2 7.8 %copy-start.10 = (f32[4096]{0:T(1024)S(1)}, f32[4096]{0:T(1024)}, u32[]{:S(2)}) copy-start(f32[4096]{0:T(1024)} %param.14) | copy-start | bytes 49156
  7.2 7.1 copy-start.11
  7.2 7.5 %copy-start.12 = (s32[2]{0:T(128)S(1)}, s32[2]{0:T(128)}, u32[]{:S(2)}) copy-start(s32[2]{0:T(128)} %param.13) | copy-start | bytes 28
  7.2 190.7 %reduce-scatter.5.cloned.1.call-start = ((), (), s32[]{:S(2)}) async-start(), calls=%async_computation.4 | async-start | bytes 4456448 | tf_op jit(solution)/shard_map/reduce_scatter | solution.py:121
  7.3 7.7 %copy-start.3 = (bf16[2,128,4096]{2,1,0:T(8,128)(2,1)S(1)}, bf16[2,128,4096]{2,1,0:T(8,128)(2,1)}, u32[]{:S(2)}) copy-start(bf16[2,128,4096]{2,1,0:T(8,128)(2,1)} %param.11) | copy-start | bytes 6291460
  15.0 2.1 copy-start.4
  15.0 2.8 copy-start.6
  17.1 33.7 %copy-start.13 = (s32[128]{0:T(128)S(1)}, s32[128]{0:T(128)}, u32[]{:S(2)}) copy-start(s32[128]{0:T(128)} %param.18) | copy-start | bytes 1540
  19.5 7.1 collective-permute-start
  20.0 6.7 collective-permute-start.8
  26.6 6.0 collective-permute-start.1
  26.7 6.0 collective-permute-start.9
  32.7 6.0 collective-permute-start.2
  32.7 6.0 collective-permute-start.10
  38.7 6.0 collective-permute-start.3
  38.8 6.0 collective-permute-start.11
  44.7 6.0 collective-permute-start.4
  44.8 6.0 collective-permute-start.12
  50.8 6.0 collective-permute-start.5
  50.8 6.0 collective-permute-start.13
  56.8 6.0 collective-permute-start.6
  56.9 41.4 %copy-start.7 = (bf16[2,8192]{1,0:T(2,128)(2,1)}, bf16[2,8192]{1,0:T(2,128)(2,1)S(1)}, u32[]{:S(2)}) copy-start(bf16[2,8192]{1,0:T(2,128)(2,1)S(1)} %collective-permute-done.13) | copy-start | bytes 98308
  56.9 41.4 %collective-permute-start.14 = (bf16[2,8192]{1,0:T(2,128)(2,1)S(1)}, bf16[2,8192]{1,0:T(2,128)(2,1)S(1)}, u32[]{:S(2)}, u32[]{:S(2)}) collective-permute-start(bf16[2,8192]{1,0:T(2,128)(2,1)S(1)} %collective-permute-done.13), channel_id=1, source_target_pairs={{0,15},{1,0},{2,1},{3,2},{4,3},{5,4},{6,5},{7,6},{8,7},{9,8},{10,9... | collective-permute-start | bytes 98312 | tf_op jit(solution)/shard_map/ppermute | solution.py:22
  62.8 35.4 %copy-start.8 = (bf16[2,8192]{1,0:T(2,128)(2,1)}, bf16[2,8192]{1,0:T(2,128)(2,1)S(1)}, u32[]{:S(2)}) copy-start(bf16[2,8192]{1,0:T(2,128)(2,1)S(1)} %collective-permute-done.6) | copy-start | bytes 98308
  62.8 36.0 %collective-permute-start.7 = (bf16[2,8192]{1,0:T(2,128)(2,1)S(1)}, bf16[2,8192]{1,0:T(2,128)(2,1)}, u32[]{:S(2)}, u32[]{:S(2)}) collective-permute-start(bf16[2,8192]{1,0:T(2,128)(2,1)S(1)} %collective-permute-done.6), channel_id=1, source_target_pairs={{0,1},{1,2},{2,3},{3,4},{4,5},{5,6},{6,7},{7,8},{8,9},{9,10},{10,1... | collective-permute-start | bytes 98312 | tf_op jit(solution)/shard_map/ppermute | solution.py:20
  98.3 0.6 copy-start.9
  112.8 5.7 copy-start.1
  127.6 219.3 %reduce-scatter.7.cloned.1.call-start = ((), (), s32[]{:S(2)}) async-start(), calls=%async_computation.5 | async-start | bytes 4456448 | tf_op jit(solution)/shard_map/reduce_scatter | solution.py:121
  277.2 69.7 %copy-start.2 = (f32[512,128]{1,0:T(8,128)S(1)}, f32[512,128]{1,0:T(8,128)}, u32[]{:S(2)}) copy-start(f32[512,128]{1,0:T(8,128)} %reduce-scatter.5.cloned.1.call-done) | copy-start | bytes 786436
  277.3 219.1 %reduce-scatter.9.cloned.1.call-start = ((), (), s32[]{:S(2)}) async-start(), calls=%async_computation.6 | async-start | bytes 4456448 | tf_op jit(solution)/shard_map/reduce_scatter | solution.py:121
  426.2 220.2 %reduce-scatter.11.cloned.1.call-start = ((), (), s32[]{:S(2)}) async-start(), calls=%async_computation.7 | async-start | bytes 4456448 | tf_op jit(solution)/shard_map/reduce_scatter | solution.py:121
  576.6 0.7 copy-start.14
  677.7 58.4 %copy-start.5 = (f32[512,128]{1,0:T(8,128)}, f32[512,128]{1,0:T(8,128)S(1)}, u32[]{:S(2)}) copy-start(f32[512,128]{1,0:T(8,128)S(1)} %fusion.21) | copy-start | bytes 786436
Sparse Core Ops, SparseCore 0:
  127.8 70.1 reduce-scatter.4
  277.4 69.5 reduce-scatter.6
  426.4 69.9 reduce-scatter.8
  576.8 69.6 reduce-scatter.10
